TPU v7x, 256 devices: a whole 4x4x8 slice. The times are simulated.
256 devices in a mesh: wide: 64 (over z_lo, x, y), narrow: 4 (over z_hi, core).
Axes of the slice: x: 4, y: 4, z: 8 (z_hi: 2, z_lo: 4; z = z_hi * 4 + z_lo), core: 2. Of those that a mesh axis runs over, the one named last changes fastest.
Arguments:
- constraint_mats: bfloat16 [1024, 256, 256], P(('narrow', 'wide')), may hold values from -0.375 to 0.375
- primal_matrix: bfloat16 [256, 256], replicated, may hold values from -0.25 to 0.25
- inverse_dual_iterate: bfloat16 [256, 256], replicated, may hold values from -0.25 to 0.25
Outputs:
- schur: float32 [1024, 1024], P(('narrow', 'wide'))
All inputs are finite; a program needn't handle non-finite values.
Results may differ from a plain program's by a relative error of at most 0.0029.
Values may be sent and summed in bfloat16 or wider, within the bound.
A program may use at most 64 MiB of HBM per device.

v0:
```python
import jax
import jax.numpy as jnp
from jax import lax
from jax.sharding import PartitionSpec as P


def contract(u_rows, constraint_row_stack):
    return lax.dot_general(
        u_rows, constraint_row_stack, (((1,), (1,)), ((), ())), preferred_element_type=jnp.float32
    )


def body(constraint_mats, primal_matrix, inverse_dual_iterate):
    count = constraint_mats.shape[0]
    order = constraint_mats.shape[1]
    wide = lax.axis_size("wide")
    left_product = jnp.einsum(
        "ab,ibc->iac", primal_matrix, constraint_mats, preferred_element_type=jnp.float32
    ).astype(jnp.bfloat16)
    product_matrices = jnp.einsum(
        "lsx,xm->lsm", left_product, inverse_dual_iterate, preferred_element_type=jnp.float32
    ).astype(jnp.bfloat16)
    u_flat = product_matrices.reshape(count, order * order)
    a_flat = constraint_mats.reshape(count, order * order)
    both = jnp.stack([u_flat, a_flat])
    pieces = lax.all_to_all(both, "wide", split_axis=2, concat_axis=1, tiled=True)
    every = lax.all_gather(pieces, "narrow", axis=1, tiled=True)
    partial_value = 0.5 * (contract(pieces[0], every[1]) + contract(pieces[1], every[0]))
    rows = partial_value.shape[0] // wide
    blocks = partial_value.reshape(wide, rows, partial_value.shape[1])
    arrived = lax.all_to_all(blocks, "wide", split_axis=0, concat_axis=0, tiled=True)
    return jnp.sum(arrived, axis=0)


def solution(mesh):
    in_specs = (P(("narrow", "wide"), None, None), P(), P())
    out_specs = P(("narrow", "wide"), None)
    return jax.shard_map(body, mesh=mesh, in_specs=in_specs, out_specs=out_specs, check_vma=False)
```

profile of v0, /device:TPU:1, one launch (start us, length us, event | category | flops | bytes accessed | tf_op | source)
XLA Modules:
  0.0 422.6 jit_solution(4422344716620643686)
XLA Ops:
  6.5 0.0 copy-start
  6.5 0.0 all-gather.2.cloned.1.call-start
  6.5 1.5 stack_reshape.7
  8.0 0.0 copy-done
  8.0 1.8 convolution_convert_fusion
  9.9 0.4 stack_reshape.6
  10.3 0.7 pad_maximum_fusion
  11.0 51.0 %copy.18 = bf16[2,4,65536]{1,0,2:T(2,128)(2,1)} copy(bf16[2,4,65536]{2,1,0:T(4,128)(2,1)S(1)} %pad_maximum_fusion) | data formatting | bytes 2097152 | tf_op jit(solution)/shard_map/stack | solution.py:25
  62.0 61.1 %reshape.10 = bf16[64,2,4096]{2,1,0:T(2,128)(2,1)S(1)} reshape(bf16[65536,2,4]{2,1,0:T(2,128)(2,1)} %bitcast.29) | data formatting | bytes 2097152
  123.2 39.6 %all_to_all.23 = bf16[64,2,4096]{2,1,0:T(2,128)(2,1)S(1)} all-to-all(bf16[64,2,4096]{2,1,0:T(2,128)(2,1)S(1)} %reshape.10), channel_id=1, replica_groups=mesh['wide'=64,'narrow'=4] {'wide'}, dimensions={0} | all-to-all | bytes 2097152 | tf_op jit(solution)/shard_map/all_to_all | solution.py:26
  162.8 73.3 %reshape.11 = bf16[65536,2,4]{2,1,0:T(2,128)(2,1)} reshape(bf16[64,2,4096]{2,1,0:T(2,128)(2,1)S(1)} %all_to_all.23) | data formatting | bytes 2097152
  236.1 65.3 %copy.19 = bf16[2,4,64,1024]{3,1,2,0:T(4,128)(2,1)S(1)} copy(bf16[2,4,64,1024]{1,0,3,2:T(2,128)(2,1)} %bitcast.30) | data formatting | bytes 2097152 | tf_op jit(solution)/shard_map/all_to_all | solution.py:26
  301.4 2.1 copy.20
  303.5 0.0 all-gather.2.cloned.1.call-update
  303.5 0.4 fusion.9
  303.9 0.1 squeeze.12
  304.0 0.1 squeeze.14
  304.1 65.0 %all-gather.2.cloned.1.call-done = bf16[2,1024,1024]{2,0,1:T(2,128)(2,1)} async-done(((bf16[2,256,1024]{2,0,1:T(2,128)(2,1)}), bf16[2,1024,1024]{2,0,1:T(2,128)(2,1)}) %all-gather.2.cloned.1.call-update) | async-done | bytes 4194320 | tf_op jit(solution)/shard_map/all_gather | solution.py:27
  369.1 8.9 %fusion.8 = (bf16[1,1024,1024]{2,0,1:T(2,128)(2,1)S(1)}, bf16[1,1024,1024]{2,0,1:T(2,128)(2,1)S(1)}) fusion(bf16[2,1024,1024]{2,0,1:T(2,128)(2,1)} %all-gather.2.cloned.1.call-done), kind=kLoop, calls=%fused_computation.12 | loop fusion | bytes 8388608 | tf_op jit(solution)/shard_map/slice | solution.py:28
  378.0 0.9 fusion
  378.9 0.0 copy-start.1
  379.0 1.0 fusion.3
  379.9 0.3 reshape.7
  380.3 34.7 %all_to_all.24 = f32[64,4,1024]{2,1,0:T(4,128)S(1)} all-to-all(f32[64,4,1024]{2,1,0:T(4,128)S(1)} %reshape.7), channel_id=1, replica_groups=mesh['wide'=64,'narrow'=4] {'wide'}, dimensions={0} | all-to-all | bytes 2097152 | tf_op jit(solution)/shard_map/all_to_all | solution.py:31
  415.0 0.8 reduce_sum.9
  415.8 0.0 copy-done.1
Async XLA Ops:
  6.5 1.5 copy-start
  6.5 362.6 %all-gather.2.cloned.1.call-start = ((), (), s32[]{:S(2)}) async-start(), calls=%async_computation.2 | async-start | bytes 5242880 | tf_op jit(solution)/shard_map/all_gather | solution.py:27
  378.9 36.8 %copy-start.1 = (bf16[256,256]{1,0:T(8,128)(2,1)S(1)}, bf16[256,256]{1,0:T(8,128)(2,1)}, u32[]{:S(2)}) copy-start(bf16[256,256]{1,0:T(8,128)(2,1)} %param.5) | copy-start | bytes 393220
Sparse Core Ops, SparseCore 0:
  303.6 65.4 all-gather.1
where the time goes:
time: 424 us; the launch traced here: 423 us
  local copies, waits for them, and re-layouts  265 us (62%)
  blocking collectives  74.3 us (18%)
  waiting for transfers between devices  65 us (15%)
  between operations  13.5 us (3%)
    unnamed x6, local copies, waits for them, and re-layouts  134 us
    all_to_all x2, local copies, waits for them, and re-layouts, body(): lax.all_to_all(both, 'wide', split_axis=2, concat_axis=1, tiled=True)  67.4 us
    all_gather x1, waiting for transfers between devices, body(): every = lax.all_gather(pieces, 'narrow', axis=1, tiled=True)  65 us
    another operation x3, local copies, waits for them, and re-layouts, body(): both = jnp.stack([u_flat, a_flat])  52.9 us
    all_to_all x1, blocking collectives, body(): lax.all_to_all(both, 'wide', split_axis=2, concat_axis=1, tiled=True)  39.6 us
    all_to_all x1, blocking collectives, body(): lax.all_to_all(blocks, 'wide', split_axis=0, concat_axis=0, tiled=True)  34.7 us
    slice x1, local copies, waits for them, and re-layouts, body(): every[1]  8.88 us
  transfers between devices with their start and end apart: 1, of which 1 were waited for; matrix products, arithmetic and copies ran while one was open for 0% of the time, Pallas kernels for 0%

commit v1 on v0

--- a/solution.py
+++ b/solution.py
@@ -2,6 +2,11 @@
 import jax.numpy as jnp
 from jax import lax
 from jax.sharding import PartitionSpec as P
+
+
+def exchange_gather(shard, axis, dim):
+    stack = jnp.stack([shard] * lax.axis_size(axis))
+    return jnp.concatenate(lax.all_to_all(stack, axis, 0, 0), axis=dim)
 
 
 def contract(u_rows, constraint_row_stack):
@@ -24,7 +29,7 @@
     a_flat = constraint_mats.reshape(count, order * order)
     both = jnp.stack([u_flat, a_flat])
     pieces = lax.all_to_all(both, "wide", split_axis=2, concat_axis=1, tiled=True)
-    every = lax.all_gather(pieces, "narrow", axis=1, tiled=True)
+    every = exchange_gather(pieces, "narrow", 1)
     partial_value = 0.5 * (contract(pieces[0], every[1]) + contract(pieces[1], every[0]))
     rows = partial_value.shape[0] // wide
     blocks = partial_value.reshape(wide, rows, partial_value.shape[1])

time: 424 us -> 442 us (1.042)
  blocking collectives: 74.3 us -> 89.6 us
  between operations: 13.5 us -> 0.12 us
  waiting for transfers between devices: 65 us -> 76.8 us
  starting transfers between devices: 0.01 us -> 8.39 us
  local copies, waits for them, and re-layouts: 265 us -> 260 us
    all_to_all x0 -> x1, waiting for transfers between devices: none -> 76.8 us  [exchange_gather(): return jnp.concatenate(lax.all_to_all(stack, axis, 0, 0), axis=dim)]
    all_gather x1 -> x0, waiting for transfers between devices: 65 us -> none  [body(): every = lax.all_gather(pieces, 'narrow', axis=1, tiled=True)]
    all_to_all x1, blocking collectives: 34.7 us -> 50 us  [body(): lax.all_to_all(blocks, 'wide', split_axis=0, concat_axis=0, tiled=True)]
    all_to_all x0 -> x1, starting transfers between devices: none -> 8.39 us  [exchange_gather(): return jnp.concatenate(lax.all_to_all(stack, axis, 0, 0), axis=dim)]
    slice x2, local copies, waits for them, and re-layouts: 9.25 us -> 3.05 us  [the longest x1 2.69 us: body(): every[0]]
where the time goes in v1:
time: 442 us; the launch traced here: 440 us
  local copies, waits for them, and re-layouts  260 us (59%)
  blocking collectives  89.6 us (20%)
  waiting for transfers between devices  76.8 us (17%)
  starting transfers between devices  8.39 us (2%)
    unnamed x6, local copies, waits for them, and re-layouts  134 us
    all_to_all x1, waiting for transfers between devices, exchange_gather(): return jnp.concatenate(lax.all_to_all(stack, axis, 0, 0), axis=dim)  76.8 us
    all_to_all x2, local copies, waits for them, and re-layouts, body(): lax.all_to_all(both, 'wide', split_axis=2, concat_axis=1, tiled=True)  66.4 us
    another operation x3, local copies, waits for them, and re-layouts, body(): both = jnp.stack([u_flat, a_flat])  52.8 us
    all_to_all x1, blocking collectives, body(): lax.all_to_all(blocks, 'wide', split_axis=0, concat_axis=0, tiled=True)  50 us
    all_to_all x1, blocking collectives, body(): lax.all_to_all(both, 'wide', split_axis=2, concat_axis=1, tiled=True)  39.6 us
  transfers between devices with their start and end apart: 1, of which 1 were waited for; matrix products, arithmetic and copies ran while one was open for 0% of the time, Pallas kernels for 0%

profile of v1, /device:TPU:1, one launch (start us, length us, event | category | flops | bytes accessed | tf_op | source)
XLA Modules:
  0.0 439.9 jit_solution(38121477208475116)
XLA Ops:
  0.0 0.0 copy-start
  0.0 1.5 stack_reshape.7
  1.5 0.0 copy-done
  1.5 1.8 convolution_convert_fusion
  3.3 0.4 stack_reshape.6
  3.7 0.7 pad_maximum_fusion
  4.5 50.9 %copy.15 = bf16[2,4,65536]{1,0,2:T(2,128)(2,1)} copy(bf16[2,4,65536]{2,1,0:T(4,128)(2,1)S(1)} %pad_maximum_fusion) | data formatting | bytes 2097152 | tf_op jit(solution)/shard_map/stack | solution.py:30
  55.4 61.1 %reshape.22 = bf16[64,2,4096]{2,1,0:T(2,128)(2,1)S(1)} reshape(bf16[65536,2,4]{2,1,0:T(2,128)(2,1)} %bitcast.24) | data formatting | bytes 2097152
  116.5 39.6 %all_to_all.25 = bf16[64,2,4096]{2,1,0:T(2,128)(2,1)S(1)} all-to-all(bf16[64,2,4096]{2,1,0:T(2,128)(2,1)S(1)} %reshape.22), channel_id=1, replica_groups=mesh['wide'=64,'narrow'=4] {'wide'}, dimensions={0} | all-to-all | bytes 2097152 | tf_op jit(solution)/shard_map/all_to_all | solution.py:31
  156.1 73.3 %reshape.23 = bf16[65536,2,4]{2,1,0:T(2,128)(2,1)} reshape(bf16[64,2,4096]{2,1,0:T(2,128)(2,1)S(1)} %all_to_all.25) | data formatting | bytes 2097152
  229.4 65.3 %copy.16 = bf16[2,4,64,1024]{3,1,2,0:T(4,128)(2,1)S(1)} copy(bf16[2,4,64,1024]{1,0,3,2:T(2,128)(2,1)} %bitcast.25) | data formatting | bytes 2097152 | tf_op jit(solution)/shard_map/all_to_all | solution.py:31
  294.8 1.1 copy.17
  295.8 0.3 copy.18
  296.1 2.5 stack.14
  298.6 8.4 %all-to-all-start.1 = ((bf16[4,2,256,1024]{3,2,1,0:T(8,128)(2,1)}), bf16[4,2,256,1024]{3,2,1,0:T(8,128)(2,1)}, u32[]{:S(2)}, u32[]{:S(2)}) async-start(bf16[4,2,256,1024]{3,2,1,0:T(8,128)(2,1)} %stack.14), calls=%async_computation.1 | async-start | bytes 8388608 | tf_op jit(solution)/shard_map/all_to_all | solution.py:9
  307.0 0.4 fusion.6
  307.4 0.1 squeeze.14
  307.5 0.1 squeeze.12
  307.6 76.8 %all-to-all-done.1 = bf16[4,2,256,1024]{3,2,1,0:T(8,128)(2,1)} async-done(((bf16[4,2,256,1024]{3,2,1,0:T(8,128)(2,1)}), bf16[4,2,256,1024]{3,2,1,0:T(8,128)(2,1)}, u32[]{:S(2)}, u32[]{:S(2)}) %all-to-all-start.1) | async-done | bytes 4194336 | tf_op jit(solution)/shard_map/all_to_all | solution.py:9
  384.5 2.7 fusion.5
  387.2 0.8 fusion.7
  388.0 0.8 fusion
  388.8 0.0 copy-start.1
  388.8 0.3 reshape.19
  389.1 50.0 %all_to_all.26 = f32[64,4,1024]{2,1,0:T(4,128)S(1)} all-to-all(f32[64,4,1024]{2,1,0:T(4,128)S(1)} %reshape.19), channel_id=1, replica_groups=mesh['wide'=64,'narrow'=4] {'wide'}, dimensions={0} | all-to-all | bytes 2097152 | tf_op jit(solution)/shard_map/all_to_all | solution.py:36
  439.1 0.8 reduce_sum.9
  439.9 0.0 copy-done.1
Async XLA Ops:
  0.0 1.5 copy-start
  298.6 85.8 %all-to-all-start.1 = ((bf16[4,2,256,1024]{3,2,1,0:T(8,128)(2,1)}), bf16[4,2,256,1024]{3,2,1,0:T(8,128)(2,1)}, u32[]{:S(2)}, u32[]{:S(2)}) async-start(bf16[4,2,256,1024]{3,2,1,0:T(8,128)(2,1)} %stack.14), calls=%async_computation.1 | async-start | bytes 8388608 | tf_op jit(solution)/shard_map/all_to_all | solution.py:9
  388.8 51.2 %copy-start.1 = (bf16[256,256]{1,0:T(8,128)(2,1)S(1)}, bf16[256,256]{1,0:T(8,128)(2,1)}, u32[]{:S(2)}) copy-start(bf16[256,256]{1,0:T(8,128)(2,1)} %param.5) | copy-start | bytes 393220

commit v2 on v0

--- a/solution.py
+++ b/solution.py
@@ -2,6 +2,13 @@
 import jax.numpy as jnp
 from jax import lax
 from jax.sharding import PartitionSpec as P
+
+
+def trade_parts(block, axis, split, join):
+    devices = lax.axis_size(axis)
+    blocks = jnp.stack(jnp.split(block, devices, axis=split), axis=0)
+    blocks = lax.all_to_all(blocks, axis, split_axis=0, concat_axis=0)
+    return jnp.concatenate(blocks, axis=join)
 
 
 def contract(u_rows, constraint_row_stack):
@@ -23,7 +30,7 @@
     u_flat = product_matrices.reshape(count, order * order)
     a_flat = constraint_mats.reshape(count, order * order)
     both = jnp.stack([u_flat, a_flat])
-    pieces = lax.all_to_all(both, "wide", split_axis=2, concat_axis=1, tiled=True)
+    pieces = trade_parts(both, "wide", 2, 1)
     every = lax.all_gather(pieces, "narrow", axis=1, tiled=True)
     partial_value = 0.5 * (contract(pieces[0], every[1]) + contract(pieces[1], every[0]))
     rows = partial_value.shape[0] // wide

time: 424 us -> 173 us (0.41)
  local copies, waits for them, and re-layouts: 265 us -> 15 us
    unnamed x6 -> x66, local copies, waits for them, and re-layouts: 134 us -> 1.14 us
    all_to_all x2 -> x0, local copies, waits for them, and re-layouts: 67.4 us -> none  [body(): lax.all_to_all(both, 'wide', split_axis=2, concat_axis=1, tiled=True)]
    another operation x3, local copies, waits for them, and re-layouts: 52.9 us -> 2.08 us  [body(): both = jnp.stack([u_flat, a_flat])]
where the time goes in v2:
time: 173 us
  blocking collectives  74.3 us (43%)
  waiting for transfers between devices  65 us (38%)
  local copies, waits for them, and re-layouts  15 us (9%)
  between operations  13.8 us (8%)
  matrix products  3.74 us (2%)
    all_gather x1, waiting for transfers between devices, body(): every = lax.all_gather(pieces, 'narrow', axis=1, tiled=True)  65 us
    all_to_all x1, blocking collectives, trade_parts(): blocks = lax.all_to_all(blocks, axis, split_axis=0, concat_axis=0)  39.6 us
    all_to_all x1, blocking collectives, body(): lax.all_to_all(blocks, 'wide', split_axis=0, concat_axis=0, tiled=True)  34.7 us
    slice x1, local copies, waits for them, and re-layouts, body(): every[1]  8.81 us
  transfers between devices with their start and end apart: 1, of which 1 were waited for; matrix products, arithmetic and copies ran while one was open for 0% of the time, Pallas kernels for 0%

profile of v2, /device:TPU:1, one launch (start us, length us, event | category | flops | bytes accessed | tf_op | source)
XLA Modules:
  0.0 172.7 jit_solution(320172197890776471)
XLA Ops:
  6.5 0.0 copy-start
  6.5 0.0 all-gather.2.cloned.1.call-start
  6.5 1.5 stack_reshape.7
  8.0 0.0 copy-done
  8.0 1.8 %convolution_convert_fusion = bf16[4,256,256]{2,1,0:T(8,128)(2,1)S(1)} fusion(bf16[4,256,256]{2,1,0:T(8,128)(2,1)} %param.3, bf16[256,256]{1,0:T(8,128)(2,1)S(1)} %copy-done, bf16[256,256]{1,0:T(8,128)(2,1)} %param.4), kind=kOutput, calls=%fused_computation.6 | convolution fusion | flops 268959744 | bytes 1310720 | tf_op jit(solution)/shard_map/lsx,xm->lsm/dot_general | solution.py:27
  9.9 0.4 stack_reshape.6
  10.3 0.2 constant_dynamic-update-slice_fusion.1
  10.5 0.2 constant_dynamic-update-slice_fusion
  12.0 39.6 %all_to_all.10 = bf16[64,2,4,1024]{3,2,1,0:T(4,128)(2,1)S(1)} all-to-all(bf16[64,2,4,1024]{3,2,1,0:T(4,128)(2,1)S(1)} %constant_dynamic-update-slice_fusion.2), channel_id=1, replica_groups=mesh['wide'=64,'narrow'=4] {'wide'}, dimensions={0} | all-to-all | bytes 2097152 | tf_op jit(solution)/shard_map/all_to_all | solution.py:10
  51.6 2.1 %copy.74 = bf16[2,64,4,1024]{3,0,2,1:T(2,128)(2,1)} copy(bf16[2,64,4,1024]{3,2,0,1:T(4,128)(2,1)S(1)} %bitcast.286) | data formatting | bytes 2097152 | tf_op jit(solution)/shard_map/reshape | solution.py:11
  53.6 0.0 all-gather.2.cloned.1.call-update
  53.7 0.4 fusion.9
  54.0 0.1 squeeze.12
  54.2 0.1 squeeze.14
  54.3 65.0 %all-gather.2.cloned.1.call-done = bf16[2,1024,1024]{2,0,1:T(2,128)(2,1)} async-done(((bf16[2,256,1024]{2,0,1:T(2,128)(2,1)}), bf16[2,1024,1024]{2,0,1:T(2,128)(2,1)}) %all-gather.2.cloned.1.call-update) | async-done | bytes 4194320 | tf_op jit(solution)/shard_map/all_gather | solution.py:34
  119.3 8.8 %fusion.8 = (bf16[1,1024,1024]{2,0,1:T(2,128)(2,1)S(1)}, bf16[1,1024,1024]{2,0,1:T(2,128)(2,1)S(1)}) fusion(bf16[2,1024,1024]{2,0,1:T(2,128)(2,1)} %all-gather.2.cloned.1.call-done), kind=kLoop, calls=%fused_computation.141 | loop fusion | bytes 8388608 | tf_op jit(solution)/shard_map/slice | solution.py:35
  128.1 0.9 fusion
  129.1 1.0 fusion.3
  130.0 0.3 reshape.15
  130.4 34.7 %all_to_all.11 = f32[64,4,1024]{2,1,0:T(4,128)S(1)} all-to-all(f32[64,4,1024]{2,1,0:T(4,128)S(1)} %reshape.15), channel_id=1, replica_groups=mesh['wide'=64,'narrow'=4] {'wide'}, dimensions={0} | all-to-all | bytes 2097152 | tf_op jit(solution)/shard_map/all_to_all | solution.py:38
  165.1 0.8 reduce_sum.9
  (64 shorter events, 1.0 us)
Async XLA Ops:
  6.5 1.5 copy-start
  6.5 112.8 %all-gather.2.cloned.1.call-start = ((), (), s32[]{:S(2)}) async-start(), calls=%async_computation.2 | async-start | bytes 5242880 | tf_op jit(solution)/shard_map/all_gather | solution.py:34
Sparse Core Ops, SparseCore 0:
  53.8 65.4 all-gather.1
